TPU v7x, 32 devices: a whole 2x2x4 slice. The times are simulated.
32 devices in a mesh: grp: 2 (over x), con: 16 (over z, y, core).
Axes of the slice: x: 2, y: 2, z: 4, core: 2. Of those that a mesh axis runs over, the one named last changes fastest.
Arguments:
- matrix: float32 [32768, 2048], P(('grp', 'con')), parts along dimension 0, may hold values from -0.046875 to 0.046875
- bounds_rhs: float32 [32768, 128], P(('grp', 'con')), parts along dimension 0, may hold values from -3 to 3
- costs: float32 [4096, 128], P(('grp', 'con')), parts along dimension 0, may hold values from -12 to 12
- upper: float32 [4096], P(('grp', 'con')), parts along dimension 0, may hold values from 0.5 to 2
- bound_mask: int32 [4096], P(('grp', 'con')), parts along dimension 0, may hold values 0 or 1
- node_map: int32 [3, 256], P(None, 'grp'), parts along dimension 1, may hold values from 0 to 63, as said below
- weights: int32 [256], P('grp'), parts along dimension 0, may hold values from 1 to 10
Outputs:
- primal: float32 [4096, 128], P(('grp', 'con')), parts along dimension 0
- dual: float32 [32768, 128], P(('grp', 'con')), parts along dimension 0
- multipliers: float32 [4096, 128], P(('grp', 'con')), parts along dimension 0
- gaps: float32 [4], P('grp'), parts along dimension 0
There are 2 independent parts, one for each index of `grp`. A program takes and returns all parts, laid end to end along the dimension named above; each array names one. Nothing has to cross between parts.
Inputs may be any that keep to these rules, and one draw needn't show every extreme that they name: `node_map`: row t numbers the 4 ** (t + 1) nodes of that section; each node holds 128 / 4 ** (t + 1) scenarios, and the nodes of row t + 1 split those of row t.
All inputs are finite; a program needn't handle non-finite values. No bound on the sum of `bound_mask` on one device may be relied on, other than what follows from the above.
Results may differ from a plain program's by a relative error of at most 0.0001.
Values sent between devices are 32-bit elements; how exact they have to be, the bound alone decides.
A program may use at most 64 MiB of HBM per device.

v0:
```python
import jax
import jax.numpy as jnp
from jax import lax
from jax.sharding import PartitionSpec as P

N = 2048
OUTER = 2
INNER = 2
highest = lax.Precision.HIGHEST
step_primal = 0.4
step_dual = 0.6
penalty = 1.0


def node_average(node_map, weights):
    weight_float = weights.astype(jnp.float32)
    probability = weight_float / jnp.sum(weight_float)
    same_node = (node_map[:, :, None] == node_map[:, None, :]).astype(jnp.float32)
    node_mass = same_node * probability[None, None, :]
    return (node_mass / jnp.sum(node_mass, axis=2, keepdims=True), probability)


def consensus(primal, averaging, column_index):
    averaged = jnp.einsum("tsr,jr->tjs", averaging, primal, precision=highest)
    section_of = column_index % (averaging.shape[0] + 1)
    section_hot = (
        section_of[None, :] == jnp.arange(averaging.shape[0], dtype=jnp.int32)[:, None]
    ).astype(jnp.float32)
    free_cols = 1.0 - jnp.sum(section_hot, axis=0)
    return jnp.sum(section_hot[:, :, None] * averaged, axis=0) + free_cols[:, None] * primal


def primal_step(primal, costs, multipliers, average, transposed, upper, flags, prox_weight):
    gradient = costs + multipliers + prox_weight * (primal - average) + transposed
    moved = jnp.maximum(primal - step_primal * gradient, 0.0)
    return jnp.where(flags[:, None] > 0, jnp.minimum(moved, upper[:, None]), moved)


def apply_rows(matrix, extrap):
    return jnp.dot(matrix, lax.all_gather(extrap, "con", axis=0, tiled=True), precision=highest)


def apply_columns(matrix, dual):
    return lax.psum_scatter(
        lax.dot_general(matrix, dual, (((0,), (0,)), ((), ())), precision=highest),
        "con",
        scatter_dimension=0,
        tiled=True,
    )


def body(matrix, bounds_rhs, costs, upper, bound_mask, node_map, weights):
    own_cols = costs.shape[0]
    scenario_count = costs.shape[1]
    averaging, probability = node_average(node_map, weights)
    start_col = lax.axis_index("con") * own_cols
    costs_all, upper_all, flags_all = (costs, upper, bound_mask.astype(jnp.float32))
    width = costs_all.shape[0]
    column_index = start_col + jnp.arange(width, dtype=jnp.int32)
    primal = jnp.zeros((width, scenario_count), jnp.float32)
    multipliers = jnp.zeros((width, scenario_count), jnp.float32)
    average = jnp.zeros((width, scenario_count), jnp.float32)
    transposed = jnp.zeros((width, scenario_count), jnp.float32)
    dual = jnp.zeros(bounds_rhs.shape, jnp.float32)
    partials = []
    for outer_turn in range(OUTER):
        prox_weight = 0.0 if outer_turn == 0 else penalty
        for inner_turn in range(INNER):
            moved = primal_step(
                primal,
                costs_all,
                multipliers,
                average,
                transposed,
                upper_all,
                flags_all,
                prox_weight,
            )
            extrap = 2.0 * moved - primal
            product = apply_rows(matrix, extrap)
            dual = jnp.maximum(dual + step_dual * (product - bounds_rhs), 0.0)
            primal = moved
            if outer_turn < OUTER - 1 or inner_turn < INNER - 1:
                transposed = apply_columns(matrix, dual)
        average = consensus(primal, averaging, column_index)
        deviation = primal - average
        multipliers = multipliers + penalty * deviation
        partial_value = jnp.sum(deviation * deviation * probability[None, :]) / N
        partial_value = lax.psum(partial_value, "con")
        partials.append(partial_value)
    gaps = jnp.stack(partials)
    return (primal, dual, multipliers, gaps)


def solution(mesh):
    placed = (
        P(("grp", "con"), None),
        P(("grp", "con"), None),
        P(("grp", "con"), None),
        P(("grp", "con")),
        P(("grp", "con")),
        P(None, "grp"),
        P("grp"),
    )
    return jax.shard_map(
        body,
        mesh=mesh,
        in_specs=placed,
        out_specs=(
            P(("grp", "con"), None),
            P(("grp", "con"), None),
            P(("grp", "con"), None),
            P("grp"),
        ),
        check_vma=False,
    )
```

profile of v0, /device:TPU:0, one launch (start us, length us, event | category | flops | bytes accessed | tf_op | source)
XLA Modules:
  0.0 413.3 jit_solution(4604648816111772595)
XLA Ops:
  7.2 0.0 all-gather.5.cloned.1.call-start
  7.2 0.7 convert_compare_fusion
  7.9 0.9 copy.23
  8.8 1.3 fusion.31
  10.1 0.0 all-gather.5.cloned.1.call-update
  10.1 0.0 reduce-scatter.4.cloned.1.call-start
  10.2 1.2 copy.25
  11.4 0.0 copy-start.2
  11.4 38.8 %all-gather.5.cloned.1.call-done = f32[2048,128]{0,1:T(8,128)} async-done(((f32[128,128]{0,1:T(8,128)}), f32[2048,128]{0,1:T(8,128)}) %all-gather.5.cloned.1.call-update) | async-done | bytes 1048592 | tf_op jit(solution)/shard_map/all_gather | solution.py:40
  50.3 12.0 %fusion.8 = f32[1024,128]{0,1:T(8,128)S(1)} fusion(f32[1024,128]{0,1:T(8,128)S(1)} %copy.25, f32[2048,128]{0,1:T(8,128)} %all-gather.5.cloned.1.call-done, f32[1024,2048]{1,0:T(8,128)} %param.7), kind=kOutput, calls=%fused_computation.15 | convolution fusion | flops 3221618688 | bytes 10485760 | tf_op jit(solution)/shard_map/dot_general | solution.py:40
  62.3 5.6 %convolution_bitcast_fusion.2 = f32[2048,128]{0,1:T(8,128)} fusion(f32[1024,128]{0,1:T(8,128)S(1)} %fusion.8, f32[1024,2048]{1,0:T(8,128)S(1)} %copy-done), kind=kOutput, calls=%fused_computation.2 | convolution fusion | flops 3221225472 | bytes 9961472 | tf_op jit(solution)/shard_map/dot_general | solution.py:45
  67.8 0.0 reduce-scatter.4.cloned.1.call-update
  67.9 0.0 all-gather.7.cloned.1.call-start
  67.9 57.0 %reduce-scatter.4.cloned.1.call-done = f32[128,128]{0,1:T(8,128)} async-done(((f32[2048,128]{0,1:T(8,128)}), f32[128,128]{0,1:T(8,128)}) %reduce-scatter.4.cloned.1.call-update) | async-done | bytes 65552 | tf_op jit(solution)/shard_map/reduce_scatter | solution.py:44
  124.9 1.5 multiply_subtract_fusion.2
  126.5 0.0 all-gather.7.cloned.1.call-update
  126.5 0.2 reduce-scatter.6.cloned.1.call-start
  126.7 37.0 %all-gather.7.cloned.1.call-done = f32[2048,128]{0,1:T(8,128)} async-done(((f32[128,128]{0,1:T(8,128)}), f32[2048,128]{0,1:T(8,128)}) %all-gather.7.cloned.1.call-update) | async-done | bytes 1048592 | tf_op jit(solution)/shard_map/all_gather | solution.py:40
  163.7 11.5 %fusion.10 = f32[1024,128]{0,1:T(8,128)S(1)} fusion(f32[1024,128]{0,1:T(8,128)S(1)} %fusion.8, f32[1024,128]{0,1:T(8,128)S(1)} %copy.25, f32[2048,128]{0,1:T(8,128)} %all-gather.7.cloned.1.call-done, f32[1024,2048]{1,0:T(8,128)} %param.7), kind=kOutput, calls=%fused_computation.17 | convolution fusion | flops 3221749760 | bytes 11010048 | tf_op jit(solution)/shard_map/dot_general | solution.py:40
  175.2 7.8 %convolution_bitcast_fusion.1 = f32[2048,128]{0,1:T(8,128)} fusion(f32[1024,128]{0,1:T(8,128)S(1)} %fusion.10, f32[1024,2048]{1,0:T(8,128)} %param.7), kind=kOutput, calls=%fused_computation.1 | convolution fusion | flops 3221225472 | bytes 9961472 | tf_op jit(solution)/shard_map/dot_general | solution.py:45
  183.0 0.0 reduce-scatter.6.cloned.1.call-update
  183.1 0.0 all-gather.9.cloned.1.call-start
  183.1 0.6 convert_reduce_fusion
  183.8 0.6 convert_divide_fusion
  184.4 0.2 select_reduce_fusion
  184.7 0.5 fusion.17
  185.2 0.1 copy.27
  185.3 54.8 %reduce-scatter.6.cloned.1.call-done = f32[128,128]{0,1:T(8,128)} async-done(((f32[2048,128]{0,1:T(8,128)}), f32[128,128]{0,1:T(8,128)}) %reduce-scatter.6.cloned.1.call-update) | async-done | bytes 65552 | tf_op jit(solution)/shard_map/reduce_scatter | solution.py:44
  240.1 1.5 multiply_subtract_fusion.1
  241.6 0.0 all-gather.9.cloned.1.call-update
  241.6 0.3 reduce-scatter.8.cloned.1.call-start
  241.9 36.7 %all-gather.9.cloned.1.call-done = f32[2048,128]{0,1:T(8,128)} async-done(((f32[128,128]{0,1:T(8,128)}), f32[2048,128]{0,1:T(8,128)}) %all-gather.9.cloned.1.call-update) | async-done | bytes 1048592 | tf_op jit(solution)/shard_map/all_gather | solution.py:40
  278.6 11.4 %fusion.12 = f32[1024,128]{0,1:T(8,128)S(1)} fusion(f32[1024,128]{0,1:T(8,128)S(1)} %fusion.10, f32[1024,128]{0,1:T(8,128)S(1)} %copy.25, f32[2048,128]{0,1:T(8,128)} %all-gather.9.cloned.1.call-done, f32[1024,2048]{1,0:T(8,128)} %param.7), kind=kOutput, calls=%fused_computation.19 | convolution fusion | flops 3221749760 | bytes 11010048 | tf_op jit(solution)/shard_map/dot_general | solution.py:40
  290.0 7.8 %convolution_bitcast_fusion = f32[2048,128]{0,1:T(8,128)} fusion(f32[1024,128]{0,1:T(8,128)S(1)} %fusion.12, f32[1024,2048]{1,0:T(8,128)} %param.7), kind=kOutput, calls=%fused_computation | convolution fusion | flops 3221225472 | bytes 9961472 | tf_op jit(solution)/shard_map/dot_general | solution.py:45
  297.9 0.0 reduce-scatter.8.cloned.1.call-update
  297.9 0.0 all-gather.11.cloned.1.call-start
  297.9 57.0 %reduce-scatter.8.cloned.1.call-done = f32[128,128]{0,1:T(8,128)} async-done(((f32[2048,128]{0,1:T(8,128)}), f32[128,128]{0,1:T(8,128)}) %reduce-scatter.8.cloned.1.call-update) | async-done | bytes 65552 | tf_op jit(solution)/shard_map/reduce_scatter | solution.py:44
  355.0 1.5 multiply_subtract_fusion
  356.5 0.0 all-gather.11.cloned.1.call-update
  356.5 0.5 fusion.18
  357.0 0.1 copy.33
  357.1 0.7 multiply_reduce_fusion.1
  359.1 31.6 %all-reduce = (f32[1]{0:T(128)}, f32[1]{0:T(128)}) all-reduce(f32[1]{0:T(128)} %bitcast.12, f32[1]{0:T(128)} %bitcast.11), channel_id=1, replica_groups=mesh['grp'=2,'con'=16] {'con'}, use_global_device_ids=true, to_apply=%region_11.12 | all-reduce | flops 2 | bytes 16 | tf_op jit(solution)/shard_map/psum | solution.py:89
  390.7 0.7 copy.34
  391.4 0.7 copy.36
  392.2 1.8 pad_maximum_fusion
  394.0 11.5 %fusion.14 = f32[1024,128]{0,1:T(8,128)S(1)} fusion(f32[1024,128]{0,1:T(8,128)S(1)} %fusion.12, f32[1024,128]{0,1:T(8,128)S(1)} %copy.25, f32[2048,128]{0,1:T(8,128)} %all-gather.11.cloned.1.call-done, f32[1024,2048]{1,0:T(8,128)} %param.7), kind=kOutput, calls=%fused_computation.21 | convolution fusion | flops 3221749760 | bytes 11010048 | tf_op jit(solution)/shard_map/dot_general | solution.py:40
  405.5 1.0 copy.35
  (12 shorter events, 0.1 us)
Async XLA Ops:
  7.2 43.1 %all-gather.5.cloned.1.call-start = ((), (), s32[]{:S(2)}) async-start(), calls=%async_computation.3 | async-start | bytes 1114112 | tf_op jit(solution)/shard_map/all_gather | solution.py:40
  10.1 114.8 %reduce-scatter.4.cloned.1.call-start = ((), (), s32[]{:S(2)}) async-start(), calls=%async_computation.4 | async-start | bytes 1114112 | tf_op jit(solution)/shard_map/reduce_scatter | solution.py:44
  11.4 113.5 %copy-start.2 = (f32[128]{0:T(128)S(1)}, f32[128]{0:T(128)}, u32[]{:S(2)}) copy-start(f32[128]{0:T(128)} %param.10) | copy-start | bytes 1540
  50.3 12.0 %copy-start = (f32[1024,2048]{1,0:T(8,128)S(1)}, f32[1024,2048]{1,0:T(8,128)}, u32[]{:S(2)}) copy-start(f32[1024,2048]{1,0:T(8,128)} %param.7) | copy-start | bytes 25165828
  67.9 95.9 %all-gather.7.cloned.1.call-start = ((), (), s32[]{:S(2)}) async-start(), calls=%async_computation.5 | async-start | bytes 1114112 | tf_op jit(solution)/shard_map/all_gather | solution.py:40
  126.5 56.7 %copy-start.3 = (s32[128]{0:T(128)S(1)}, s32[128]{0:T(128)}, u32[]{:S(2)}) copy-start(s32[128]{0:T(128)} %param.13) | copy-start | bytes 1540
  126.5 57.9 %copy-start.1 = (s32[3,128]{1,0:T(4,128)S(1)}, s32[3,128]{1,0:T(4,128)}, u32[]{:S(2)}) copy-start(s32[3,128]{1,0:T(4,128)} %param.12) | copy-start | bytes 4612
  126.5 113.6 %reduce-scatter.6.cloned.1.call-start = ((), (), s32[]{:S(2)}) async-start(), calls=%async_computation.6 | async-start | bytes 1114112 | tf_op jit(solution)/shard_map/reduce_scatter | solution.py:44
  183.1 95.5 %all-gather.9.cloned.1.call-start = ((), (), s32[]{:S(2)}) async-start(), calls=%async_computation.7 | async-start | bytes 1114112 | tf_op jit(solution)/shard_map/all_gather | solution.py:40
  241.6 113.4 %reduce-scatter.8.cloned.1.call-start = ((), (), s32[]{:S(2)}) async-start(), calls=%async_computation.8 | async-start | bytes 1114112 | tf_op jit(solution)/shard_map/reduce_scatter | solution.py:44
  297.9 96.1 %all-gather.11.cloned.1.call-start = ((), (), s32[]{:S(2)}) async-start(), calls=%async_computation.9 | async-start | bytes 1114112 | tf_op jit(solution)/shard_map/all_gather | solution.py:40
Sparse Core Ops, SparseCore 0:
  10.7 39.4 all-gather.4
  68.0 56.8 reduce-scatter.3
  127.9 35.7 all-gather.6
  183.2 56.8 reduce-scatter.5
  242.7 35.8 all-gather.8
  298.0 56.9 reduce-scatter.7
  357.9 35.7 all-gather.10
where the time goes:
time: 414 us; the launch traced here: 413 us
  waiting for transfers between devices  281 us (68%)
  matrix products  68.6 us (17%)
  blocking collectives  31.6 us (8%)
  between operations  15.6 us (4%)
  other arithmetic  10.5 us (3%)
  local copies, waits for them, and re-layouts  4.82 us (1%)
    reduce_scatter x3, waiting for transfers between devices, apply_columns(): lax.psum_scatter(lax.dot_general(matrix, dual, (((0,), (0,)), ((), ())),...  169 us
    all_gather x4, waiting for transfers between devices, apply_rows(): lax.all_gather(extrap, 'con', axis=0, tiled=True)  112 us
    dot_general x4, matrix products, apply_rows(): jnp.dot(matrix, lax.all_gather(extrap, 'con', axis=0, tiled=True), precis...  46.3 us
    psum x1, blocking collectives, body(): partial_value = lax.psum(partial_value, 'con')  31.6 us
    dot_general x3, matrix products, apply_columns(): lax.dot_general(matrix, dual, (((0,), (0,)), ((), ())), precision=highest)  21.3 us
  transfers between devices with their start and end apart: 7, of which 6 were waited for; matrix products, arithmetic and copies ran while one was open for 2% of the time, Pallas kernels for 0%

commit v1 on v0

--- a/solution.py
+++ b/solution.py
@@ -10,6 +10,28 @@
 step_primal = 0.4
 step_dual = 0.6
 penalty = 1.0
+
+
+def joined_along(tiles, dim):
+    lengths = list(tiles.shape[1:])
+    lengths[dim] *= tiles.shape[0]
+    return jnp.moveaxis(tiles, 0, dim).reshape(lengths)
+
+
+def gather_around(array, axis, dim):
+    peers = lax.axis_size(axis)
+    pairs = [(i, (i + 1) % peers) for i in range(peers)]
+    back = [(b, a) for a, b in pairs]
+    lower, upper = ([], [])
+    for step in range(peers - 1):
+        if step % 2 == 0:
+            lower.append(lax.ppermute(lower[-1] if lower else array, axis, pairs))
+        else:
+            upper.append(lax.ppermute(upper[-1] if upper else array, axis, back))
+    blocks = jnp.stack([*lower[::-1], array, *upper])
+    shift = lax.axis_index(axis) - len(lower)
+    blocks = blocks[(jnp.arange(peers) - shift) % peers]
+    return joined_along(blocks, dim)
 
 
 def node_average(node_map, weights):
@@ -37,7 +59,7 @@
 
 
 def apply_rows(matrix, extrap):
-    return jnp.dot(matrix, lax.all_gather(extrap, "con", axis=0, tiled=True), precision=highest)
+    return jnp.dot(matrix, gather_around(extrap, "con", 0), precision=highest)
 
 
 def apply_columns(matrix, dual):

time: 414 us -> 513 us (1.24)
  starting transfers between devices: 0.69 us -> 122 us
  waiting for transfers between devices: 281 us -> 247 us
  local copies, waits for them, and re-layouts: 4.82 us -> 21.2 us
  matrix products: 68.6 us -> 63.1 us
    ppermute x0 -> x60, starting transfers between devices: none -> 122 us  [the longest x28 120 us: gather_around(): upper.append(lax.ppermute(upper[-1] if upper else array, axis, back))]
    all_gather x4 -> x0, waiting for transfers between devices: 112 us -> none  [apply_rows(): lax.all_gather(extrap, 'con', axis=0, tiled=True)]
    ppermute x0 -> x60, waiting for transfers between devices: none -> 76.5 us  [the longest x32 72.1 us: gather_around(): lower.append(lax.ppermute(lower[-1] if lower else array, axis, pairs))]
    unnamed x13 -> x70, local copies, waits for them, and re-layouts: 4.64 us -> 14.4 us
    dot_general x4, matrix products: 46.3 us -> 38.5 us  [apply_rows(): return jnp.dot(matrix, gather_around(extrap, 'con', 0), precision=highest)]
    gather x0 -> x8, local copies, waits for them, and re-layouts: none -> 6 us  [gather_around(): blocks = blocks[(jnp.arange(peers) - shift) % peers]]
  transfers between devices with their start and end apart: 7 -> 63, of which waited for: 6 -> 38; matrix products, arithmetic and copies ran while one was open for 2% -> 4% of each run, Pallas kernels for 0% -> 0%
where the time goes in v1:
time: 513 us
  waiting for transfers between devices  247 us (48%)
  starting transfers between devices  122 us (24%)
  matrix products  63.1 us (12%)
  blocking collectives  35.7 us (7%)
  local copies, waits for them, and re-layouts  21.2 us (4%)
  between operations  15.7 us (3%)
  other arithmetic  8.7 us (2%)
    reduce_scatter x3, waiting for transfers between devices, apply_columns(): lax.psum_scatter(lax.dot_general(matrix, dual, (((0,), (0,)), ((), ())),...  170 us
    ppermute x28, starting transfers between devices, gather_around(): upper.append(lax.ppermute(upper[-1] if upper else array, axis, back))  120 us
    ppermute x32, waiting for transfers between devices, gather_around(): lower.append(lax.ppermute(lower[-1] if lower else array, axis, pairs))  72.1 us
    dot_general x4, matrix products, apply_rows(): return jnp.dot(matrix, gather_around(extrap, 'con', 0), precision=highest)  38.5 us
    psum x1, blocking collectives, body(): partial_value = lax.psum(partial_value, 'con')  35.7 us
    dot_general x3, matrix products, apply_columns(): lax.dot_general(matrix, dual, (((0,), (0,)), ((), ())), precision=highest)  23.5 us
    unnamed x70, local copies, waits for them, and re-layouts  14.4 us
  transfers between devices with their start and end apart: 63, of which 38 were waited for; matrix products, arithmetic and copies ran while one was open for 4% of the time, Pallas kernels for 0%

profile of v1, /device:TPU:0, one launch (start us, length us, event | category | flops | bytes accessed | tf_op | source)
XLA Modules:
  0.0 512.8 jit_solution(6232304768342384563)
XLA Ops:
  10.0 6.9 %collective-permute-done = f32[128,128]{0,1:T(8,128)S(1)} collective-permute-done((f32[128,128]{0,1:T(8,128)S(1)}, f32[128,128]{0,1:T(8,128)S(1)}, u32[]{:S(2)}, u32[]{:S(2)}) %collective-permute-start) | collective-permute-done | bytes 65568 | tf_op jit(solution)/shard_map/ppermute | solution.py:28
  16.9 4.4 collective-permute-start.8
  21.4 2.0 collective-permute-done.1
  23.3 4.4 collective-permute-start.9
  29.7 4.5 collective-permute-start.10
  36.1 4.5 collective-permute-start.11
  40.6 1.9 collective-permute-done.4
  43.8 4.5 collective-permute-start.12
  50.2 4.5 collective-permute-start.13
  56.6 4.5 collective-permute-start.14
  64.0 9.5 %fusion.8 = f32[1024,128]{0,1:T(8,128)S(1)} fusion(f32[1024,128]{0,1:T(8,128)S(1)} %copy.42, f32[2048,128]{1,0:T(8,128)S(1)} %bitcast.212, f32[1024,2048]{1,0:T(8,128)} %param.7), kind=kOutput, calls=%fused_computation.19 | convolution fusion | flops 3221618688 | bytes 10485760 | tf_op jit(solution)/shard_map/dot_general | solution.py:62
  73.5 7.8 %convolution_bitcast_fusion.2 = f32[2048,128]{0,1:T(8,128)} fusion(f32[1024,128]{0,1:T(8,128)S(1)} %fusion.8, f32[1024,2048]{1,0:T(8,128)} %param.7), kind=kOutput, calls=%fused_computation.6 | convolution fusion | flops 3221225472 | bytes 9961472 | tf_op jit(solution)/shard_map/dot_general | solution.py:67
  81.4 59.2 %reduce-scatter.4.cloned.1.call-done = f32[128,128]{0,1:T(8,128)} async-done(((f32[2048,128]{0,1:T(8,128)}), f32[128,128]{0,1:T(8,128)}) %reduce-scatter.4.cloned.1.call-update) | async-done | bytes 65552 | tf_op jit(solution)/shard_map/reduce_scatter | solution.py:66
  141.6 6.4 %collective-permute-done.15 = f32[128,128]{0,1:T(8,128)S(1)} collective-permute-done((f32[128,128]{0,1:T(8,128)S(1)}, f32[128,128]{0,1:T(8,128)S(1)}, u32[]{:S(2)}, u32[]{:S(2)}) %collective-permute-start.15) | collective-permute-done | bytes 65568 | tf_op jit(solution)/shard_map/ppermute | solution.py:28
  148.0 4.4 collective-permute-start.23
  152.4 2.0 collective-permute-done.16
  154.5 4.4 collective-permute-start.24
  160.9 4.5 collective-permute-start.25
  167.3 4.5 collective-permute-start.26
  173.7 4.5 collective-permute-start.27
  180.0 4.5 collective-permute-start.28
  186.4 4.5 collective-permute-start.29
  194.0 9.6 %fusion.10 = f32[1024,128]{0,1:T(8,128)S(1)} fusion(f32[1024,128]{0,1:T(8,128)S(1)} %fusion.8, f32[1024,128]{0,1:T(8,128)S(1)} %copy.42, f32[2048,128]{1,0:T(8,128)S(1)} %bitcast.214, f32[1024,2048]{1,0:T(8,128)} %param.7), kind=kOutput, calls=%fused_computation.21 | convolution fusion | flops 3221749760 | bytes 11010048 | tf_op jit(solution)/shard_map/dot_general | solution.py:62
  203.6 7.8 %convolution_bitcast_fusion.1 = f32[2048,128]{0,1:T(8,128)} fusion(f32[1024,128]{0,1:T(8,128)S(1)} %fusion.10, f32[1024,2048]{1,0:T(8,128)} %param.7), kind=kOutput, calls=%fused_computation.5 | convolution fusion | flops 3221225472 | bytes 9961472 | tf_op jit(solution)/shard_map/dot_general | solution.py:67
  213.7 56.2 %reduce-scatter.6.cloned.1.call-done = f32[128,128]{0,1:T(8,128)} async-done(((f32[2048,128]{0,1:T(8,128)}), f32[128,128]{0,1:T(8,128)}) %reduce-scatter.6.cloned.1.call-update) | async-done | bytes 65552 | tf_op jit(solution)/shard_map/reduce_scatter | solution.py:66
  270.9 6.4 %collective-permute-done.30 = f32[128,128]{0,1:T(8,128)S(1)} collective-permute-done((f32[128,128]{0,1:T(8,128)S(1)}, f32[128,128]{0,1:T(8,128)S(1)}, u32[]{:S(2)}, u32[]{:S(2)}) %collective-permute-start.30) | collective-permute-done | bytes 65568 | tf_op jit(solution)/shard_map/ppermute | solution.py:28
  277.3 4.4 collective-permute-start.38
  281.7 2.0 collective-permute-done.31
  283.8 4.4 collective-permute-start.39
  290.1 4.5 collective-permute-start.40
  296.6 4.5 collective-permute-start.41
  302.9 4.5 collective-permute-start.42
  309.3 4.5 collective-permute-start.43
  315.7 4.5 collective-permute-start.44
  335.3 9.9 %fusion.12 = f32[1024,128]{0,1:T(8,128)S(1)} fusion(f32[1024,128]{0,1:T(8,128)S(1)} %fusion.10, f32[1024,128]{0,1:T(8,128)S(1)} %copy.42, f32[2048,128]{1,0:T(8,128)} %bitcast.215, f32[1024,2048]{1,0:T(8,128)} %param.7), kind=kOutput, calls=%fused_computation.23 | convolution fusion | flops 3221749760 | bytes 11010048 | tf_op jit(solution)/shard_map/dot_general | solution.py:62
  345.2 7.8 %convolution_bitcast_fusion = f32[2048,128]{0,1:T(8,128)} fusion(f32[1024,128]{0,1:T(8,128)S(1)} %fusion.12, f32[1024,2048]{1,0:T(8,128)} %param.7), kind=kOutput, calls=%fused_computation.4 | convolution fusion | flops 3221225472 | bytes 9961472 | tf_op jit(solution)/shard_map/dot_general | solution.py:67
  353.1 54.8 %reduce-scatter.8.cloned.1.call-done = f32[128,128]{0,1:T(8,128)} async-done(((f32[2048,128]{0,1:T(8,128)}), f32[128,128]{0,1:T(8,128)}) %reduce-scatter.8.cloned.1.call-update) | async-done | bytes 65552 | tf_op jit(solution)/shard_map/reduce_scatter | solution.py:66
  408.8 6.4 %collective-permute-done.45 = f32[128,128]{0,1:T(8,128)S(1)} collective-permute-done((f32[128,128]{0,1:T(8,128)S(1)}, f32[128,128]{0,1:T(8,128)S(1)}, u32[]{:S(2)}, u32[]{:S(2)}) %collective-permute-start.45) | collective-permute-done | bytes 65568 | tf_op jit(solution)/shard_map/ppermute | solution.py:28
  415.2 4.4 collective-permute-start.53
  419.6 2.0 collective-permute-done.46
  421.7 4.4 collective-permute-start.54
  428.1 4.5 collective-permute-start.55
  434.5 4.5 collective-permute-start.56
  439.0 2.0 collective-permute-done.49
  441.6 4.5 collective-permute-start.57
  449.3 35.7 %all-reduce = (f32[1]{0:T(128)}, f32[1]{0:T(128)}) all-reduce(f32[1]{0:T(128)} %bitcast.81, f32[1]{0:T(128)} %bitcast.80), channel_id=1, replica_groups=mesh['grp'=2,'con'=16] {'con'}, use_global_device_ids=true, to_apply=%region_11.12 | all-reduce | flops 2 | bytes 16 | tf_op jit(solution)/shard_map/psum | solution.py:111
  488.8 4.0 collective-permute-start.59
  495.7 9.6 %fusion.14 = f32[1024,128]{0,1:T(8,128)S(1)} fusion(f32[1024,128]{0,1:T(8,128)S(1)} %fusion.12, f32[1024,128]{0,1:T(8,128)S(1)} %copy.42, f32[2048,128]{1,0:T(8,128)S(1)} %bitcast.213, f32[1024,2048]{1,0:T(8,128)} %param.7), kind=kOutput, calls=%fused_computation.25 | convolution fusion | flops 3221749760 | bytes 11010048 | tf_op jit(solution)/shard_map/dot_general | solution.py:62
  (192 shorter events, 70.7 us)
Async XLA Ops:
  7.2 133.5 %reduce-scatter.4.cloned.1.call-start = ((), (), s32[]{:S(2)}) async-start(), calls=%async_computation.3 | async-start | bytes 1114112 | tf_op jit(solution)/shard_map/reduce_scatter | solution.py:66
  9.5 7.4 %collective-permute-start = (f32[128,128]{0,1:T(8,128)S(1)}, f32[128,128]{0,1:T(8,128)S(1)}, u32[]{:S(2)}, u32[]{:S(2)}) collective-permute-start(f32[128,128]{0,1:T(8,128)S(1)} %fusion.31), channel_id=1, source_target_pairs={{0,1},{1,2},{2,3},{3,4},{4,5},{5,6},{6,7},{7,8},{8,9},{9,10},{10,1... | collective-permute-start | bytes 196616 | tf_op jit(solution)/shard_map/ppermute | solution.py:28
  16.9 6.4 %collective-permute-start.1 = (f32[128,128]{0,1:T(8,128)S(1)}, f32[128,128]{0,1:T(8,128)S(1)}, u32[]{:S(2)}, u32[]{:S(2)}) collective-permute-start(f32[128,128]{0,1:T(8,128)S(1)} %collective-permute-done), channel_id=1, source_target_pairs={{0,1},{1,2},{2,3},{3,4},{4,5},{5,6},{6,7},{7,8},{8,9},{9,10},{10,1... | collective-permute-start | bytes 196616 | tf_op jit(solution)/shard_map/ppermute | solution.py:28
  16.9 6.4 %collective-permute-start.8 = (f32[128,128]{0,1:T(8,128)S(1)}, f32[128,128]{0,1:T(8,128)S(1)}, u32[]{:S(2)}, u32[]{:S(2)}) collective-permute-start(f32[128,128]{0,1:T(8,128)S(1)} %fusion.31), channel_id=1, source_target_pairs={{1,0},{2,1},{3,2},{4,3},{5,4},{6,5},{7,6},{8,7},{9,8},{10,9},{11,1... | collective-permute-start | bytes 196616 | tf_op jit(solution)/shard_map/ppermute | solution.py:30
  23.3 6.4 %collective-permute-start.9 = (f32[128,128]{0,1:T(8,128)S(1)}, f32[128,128]{0,1:T(8,128)S(1)}, u32[]{:S(2)}, u32[]{:S(2)}) collective-permute-start(f32[128,128]{0,1:T(8,128)S(1)} %collective-permute-done.8), channel_id=1, source_target_pairs={{1,0},{2,1},{3,2},{4,3},{5,4},{6,5},{7,6},{8,7},{9,8},{10,9},{11,1... | collective-permute-start | bytes 196616 | tf_op jit(solution)/shard_map/ppermute | solution.py:30
  29.7 6.4 %collective-permute-start.10 = (f32[128,128]{0,1:T(8,128)S(1)}, f32[128,128]{0,1:T(8,128)S(1)}, u32[]{:S(2)}, u32[]{:S(2)}) collective-permute-start(f32[128,128]{0,1:T(8,128)S(1)} %collective-permute-done.9), channel_id=1, source_target_pairs={{1,0},{2,1},{3,2},{4,3},{5,4},{6,5},{7,6},{8,7},{9,8},{10,9},{11,1... | collective-permute-start | bytes 196616 | tf_op jit(solution)/shard_map/ppermute | solution.py:30
  36.1 6.5 %collective-permute-start.4 = (f32[128,128]{0,1:T(8,128)S(1)}, f32[128,128]{0,1:T(8,128)S(1)}, u32[]{:S(2)}, u32[]{:S(2)}) collective-permute-start(f32[128,128]{0,1:T(8,128)S(1)} %collective-permute-done.3), channel_id=1, source_target_pairs={{0,1},{1,2},{2,3},{3,4},{4,5},{5,6},{6,7},{7,8},{8,9},{9,10},{10,1... | collective-permute-start | bytes 196616 | tf_op jit(solution)/shard_map/ppermute | solution.py:28
  36.1 7.7 %collective-permute-start.11 = (f32[128,128]{0,1:T(8,128)S(1)}, f32[128,128]{0,1:T(8,128)S(1)}, u32[]{:S(2)}, u32[]{:S(2)}) collective-permute-start(f32[128,128]{0,1:T(8,128)S(1)} %collective-permute-done.10), channel_id=1, source_target_pairs={{1,0},{2,1},{3,2},{4,3},{5,4},{6,5},{7,6},{8,7},{9,8},{10,9},{11,1... | collective-permute-start | bytes 196616 | tf_op jit(solution)/shard_map/ppermute | solution.py:30
  42.6 6.4 %collective-permute-start.5 = (f32[128,128]{0,1:T(8,128)S(1)}, f32[128,128]{0,1:T(8,128)S(1)}, u32[]{:S(2)}, u32[]{:S(2)}) collective-permute-start(f32[128,128]{0,1:T(8,128)S(1)} %collective-permute-done.4), channel_id=1, source_target_pairs={{0,1},{1,2},{2,3},{3,4},{4,5},{5,6},{6,7},{7,8},{8,9},{9,10},{10,1... | collective-permute-start | bytes 196616 | tf_op jit(solution)/shard_map/ppermute | solution.py:28
  43.8 6.4 %collective-permute-start.12 = (f32[128,128]{0,1:T(8,128)S(1)}, f32[128,128]{0,1:T(8,128)S(1)}, u32[]{:S(2)}, u32[]{:S(2)}) collective-permute-start(f32[128,128]{0,1:T(8,128)S(1)} %collective-permute-done.11), channel_id=1, source_target_pairs={{1,0},{2,1},{3,2},{4,3},{5,4},{6,5},{7,6},{8,7},{9,8},{10,9},{11,1... | collective-permute-start | bytes 196616 | tf_op jit(solution)/shard_map/ppermute | solution.py:30
  49.0 6.4 %collective-permute-start.6 = (f32[128,128]{0,1:T(8,128)S(1)}, f32[128,128]{0,1:T(8,128)S(1)}, u32[]{:S(2)}, u32[]{:S(2)}) collective-permute-start(f32[128,128]{0,1:T(8,128)S(1)} %collective-permute-done.5), channel_id=1, source_target_pairs={{0,1},{1,2},{2,3},{3,4},{4,5},{5,6},{6,7},{7,8},{8,9},{9,10},{10,1... | collective-permute-start | bytes 196616 | tf_op jit(solution)/shard_map/ppermute | solution.py:28
  50.2 6.4 %collective-permute-start.13 = (f32[128,128]{0,1:T(8,128)S(1)}, f32[128,128]{0,1:T(8,128)S(1)}, u32[]{:S(2)}, u32[]{:S(2)}) collective-permute-start(f32[128,128]{0,1:T(8,128)S(1)} %collective-permute-done.12), channel_id=1, source_target_pairs={{1,0},{2,1},{3,2},{4,3},{5,4},{6,5},{7,6},{8,7},{9,8},{10,9},{11,1... | collective-permute-start | bytes 196616 | tf_op jit(solution)/shard_map/ppermute | solution.py:30
  55.5 6.4 %collective-permute-start.7 = (f32[128,128]{0,1:T(8,128)S(1)}, f32[128,128]{0,1:T(8,128)S(1)}, u32[]{:S(2)}, u32[]{:S(2)}) collective-permute-start(f32[128,128]{0,1:T(8,128)S(1)} %collective-permute-done.6), channel_id=1, source_target_pairs={{0,1},{1,2},{2,3},{3,4},{4,5},{5,6},{6,7},{7,8},{8,9},{9,10},{10,1... | collective-permute-start | bytes 196616 | tf_op jit(solution)/shard_map/ppermute | solution.py:28
  81.4 188.5 %reduce-scatter.6.cloned.1.call-start = ((), (), s32[]{:S(2)}) async-start(), calls=%async_computation.4 | async-start | bytes 1114112 | tf_op jit(solution)/shard_map/reduce_scatter | solution.py:66
  141.5 6.4 %collective-permute-start.15 = (f32[128,128]{0,1:T(8,128)S(1)}, f32[128,128]{0,1:T(8,128)S(1)}, u32[]{:S(2)}, u32[]{:S(2)}) collective-permute-start(f32[128,128]{0,1:T(8,128)S(1)} %get-tuple-element.26), channel_id=1, source_target_pairs={{0,1},{1,2},{2,3},{3,4},{4,5},{5,6},{6,7},{7,8},{8,9},{9,10},{10,1... | collective-permute-start | bytes 196616 | tf_op jit(solution)/shard_map/ppermute | solution.py:28
  148.0 6.5 %collective-permute-start.16 = (f32[128,128]{0,1:T(8,128)S(1)}, f32[128,128]{0,1:T(8,128)S(1)}, u32[]{:S(2)}, u32[]{:S(2)}) collective-permute-start(f32[128,128]{0,1:T(8,128)S(1)} %collective-permute-done.15), channel_id=1, source_target_pairs={{0,1},{1,2},{2,3},{3,4},{4,5},{5,6},{6,7},{7,8},{8,9},{9,10},{10,1... | collective-permute-start | bytes 196616 | tf_op jit(solution)/shard_map/ppermute | solution.py:28
  148.0 6.5 %collective-permute-start.23 = (f32[128,128]{0,1:T(8,128)S(1)}, f32[128,128]{0,1:T(8,128)S(1)}, u32[]{:S(2)}, u32[]{:S(2)}) collective-permute-start(f32[128,128]{0,1:T(8,128)S(1)} %get-tuple-element.26), channel_id=1, source_target_pairs={{1,0},{2,1},{3,2},{4,3},{5,4},{6,5},{7,6},{8,7},{9,8},{10,9},{11,1... | collective-permute-start | bytes 196616 | tf_op jit(solution)/shard_map/ppermute | solution.py:30
  154.5 6.4 %collective-permute-start.17 = (f32[128,128]{0,1:T(8,128)S(1)}, f32[128,128]{0,1:T(8,128)S(1)}, u32[]{:S(2)}, u32[]{:S(2)}) collective-permute-start(f32[128,128]{0,1:T(8,128)S(1)} %collective-permute-done.16), channel_id=1, source_target_pairs={{0,1},{1,2},{2,3},{3,4},{4,5},{5,6},{6,7},{7,8},{8,9},{9,10},{10,1... | collective-permute-start | bytes 196616 | tf_op jit(solution)/shard_map/ppermute | solution.py:28
  154.5 6.4 %collective-permute-start.24 = (f32[128,128]{0,1:T(8,128)S(1)}, f32[128,128]{0,1:T(8,128)S(1)}, u32[]{:S(2)}, u32[]{:S(2)}) collective-permute-start(f32[128,128]{0,1:T(8,128)S(1)} %collective-permute-done.23), channel_id=1, source_target_pairs={{1,0},{2,1},{3,2},{4,3},{5,4},{6,5},{7,6},{8,7},{9,8},{10,9},{11,1... | collective-permute-start | bytes 196616 | tf_op jit(solution)/shard_map/ppermute | solution.py:30
  160.9 6.4 %collective-permute-start.18 = (f32[128,128]{0,1:T(8,128)S(1)}, f32[128,128]{0,1:T(8,128)S(1)}, u32[]{:S(2)}, u32[]{:S(2)}) collective-permute-start(f32[128,128]{0,1:T(8,128)S(1)} %collective-permute-done.17), channel_id=1, source_target_pairs={{0,1},{1,2},{2,3},{3,4},{4,5},{5,6},{6,7},{7,8},{8,9},{9,10},{10,1... | collective-permute-start | bytes 196616 | tf_op jit(solution)/shard_map/ppermute | solution.py:28
  160.9 6.4 %collective-permute-start.25 = (f32[128,128]{0,1:T(8,128)S(1)}, f32[128,128]{0,1:T(8,128)S(1)}, u32[]{:S(2)}, u32[]{:S(2)}) collective-permute-start(f32[128,128]{0,1:T(8,128)S(1)} %collective-permute-done.24), channel_id=1, source_target_pairs={{1,0},{2,1},{3,2},{4,3},{5,4},{6,5},{7,6},{8,7},{9,8},{10,9},{11,1... | collective-permute-start | bytes 196616 | tf_op jit(solution)/shard_map/ppermute | solution.py:30
  167.2 6.4 %collective-permute-start.19 = (f32[128,128]{0,1:T(8,128)S(1)}, f32[128,128]{0,1:T(8,128)S(1)}, u32[]{:S(2)}, u32[]{:S(2)}) collective-permute-start(f32[128,128]{0,1:T(8,128)S(1)} %collective-permute-done.18), channel_id=1, source_target_pairs={{0,1},{1,2},{2,3},{3,4},{4,5},{5,6},{6,7},{7,8},{8,9},{9,10},{10,1... | collective-permute-start | bytes 196616 | tf_op jit(solution)/shard_map/ppermute | solution.py:28
  167.3 6.4 %collective-permute-start.26 = (f32[128,128]{0,1:T(8,128)S(1)}, f32[128,128]{0,1:T(8,128)S(1)}, u32[]{:S(2)}, u32[]{:S(2)}) collective-permute-start(f32[128,128]{0,1:T(8,128)S(1)} %collective-permute-done.25), channel_id=1, source_target_pairs={{1,0},{2,1},{3,2},{4,3},{5,4},{6,5},{7,6},{8,7},{9,8},{10,9},{11,1... | collective-permute-start | bytes 196616 | tf_op jit(solution)/shard_map/ppermute | solution.py:30
  173.6 6.4 %collective-permute-start.20 = (f32[128,128]{0,1:T(8,128)S(1)}, f32[128,128]{0,1:T(8,128)S(1)}, u32[]{:S(2)}, u32[]{:S(2)}) collective-permute-start(f32[128,128]{0,1:T(8,128)S(1)} %collective-permute-done.19), channel_id=1, source_target_pairs={{0,1},{1,2},{2,3},{3,4},{4,5},{5,6},{6,7},{7,8},{8,9},{9,10},{10,1... | collective-permute-start | bytes 196616 | tf_op jit(solution)/shard_map/ppermute | solution.py:28
  173.7 6.4 %collective-permute-start.27 = (f32[128,128]{0,1:T(8,128)S(1)}, f32[128,128]{0,1:T(8,128)S(1)}, u32[]{:S(2)}, u32[]{:S(2)}) collective-permute-start(f32[128,128]{0,1:T(8,128)S(1)} %collective-permute-done.26), channel_id=1, source_target_pairs={{1,0},{2,1},{3,2},{4,3},{5,4},{6,5},{7,6},{8,7},{9,8},{10,9},{11,1... | collective-permute-start | bytes 196616 | tf_op jit(solution)/shard_map/ppermute | solution.py:30
  180.0 6.4 %collective-permute-start.21 = (f32[128,128]{0,1:T(8,128)S(1)}, f32[128,128]{0,1:T(8,128)S(1)}, u32[]{:S(2)}, u32[]{:S(2)}) collective-permute-start(f32[128,128]{0,1:T(8,128)S(1)} %collective-permute-done.20), channel_id=1, source_target_pairs={{0,1},{1,2},{2,3},{3,4},{4,5},{5,6},{6,7},{7,8},{8,9},{9,10},{10,1... | collective-permute-start | bytes 196616 | tf_op jit(solution)/shard_map/ppermute | solution.py:28
  180.0 6.4 %collective-permute-start.28 = (f32[128,128]{0,1:T(8,128)S(1)}, f32[128,128]{0,1:T(8,128)S(1)}, u32[]{:S(2)}, u32[]{:S(2)}) collective-permute-start(f32[128,128]{0,1:T(8,128)S(1)} %collective-permute-done.27), channel_id=1, source_target_pairs={{1,0},{2,1},{3,2},{4,3},{5,4},{6,5},{7,6},{8,7},{9,8},{10,9},{11,1... | collective-permute-start | bytes 196616 | tf_op jit(solution)/shard_map/ppermute | solution.py:30
  186.4 6.6 %collective-permute-start.29 = (f32[128,128]{0,1:T(8,128)S(1)}, f32[128,128]{0,1:T(8,128)S(1)}, u32[]{:S(2)}, u32[]{:S(2)}) collective-permute-start(f32[128,128]{0,1:T(8,128)S(1)} %collective-permute-done.28), channel_id=1, source_target_pairs={{1,0},{2,1},{3,2},{4,3},{5,4},{6,5},{7,6},{8,7},{9,8},{10,9},{11,1... | collective-permute-start | bytes 196616 | tf_op jit(solution)/shard_map/ppermute | solution.py:30
  211.5 196.4 %reduce-scatter.8.cloned.1.call-start = ((), (), s32[]{:S(2)}) async-start(), calls=%async_computation.5 | async-start | bytes 1114112 | tf_op jit(solution)/shard_map/reduce_scatter | solution.py:66
  270.8 6.4 %collective-permute-start.30 = (f32[128,128]{0,1:T(8,128)S(1)}, f32[128,128]{0,1:T(8,128)S(1)}, u32[]{:S(2)}, u32[]{:S(2)}) collective-permute-start(f32[128,128]{0,1:T(8,128)S(1)} %get-tuple-element.22), channel_id=1, source_target_pairs={{0,1},{1,2},{2,3},{3,4},{4,5},{5,6},{6,7},{7,8},{8,9},{9,10},{10,1... | collective-permute-start | bytes 196616 | tf_op jit(solution)/shard_map/ppermute | solution.py:28
  277.3 6.5 %collective-permute-start.31 = (f32[128,128]{0,1:T(8,128)S(1)}, f32[128,128]{0,1:T(8,128)S(1)}, u32[]{:S(2)}, u32[]{:S(2)}) collective-permute-start(f32[128,128]{0,1:T(8,128)S(1)} %collective-permute-done.30), channel_id=1, source_target_pairs={{0,1},{1,2},{2,3},{3,4},{4,5},{5,6},{6,7},{7,8},{8,9},{9,10},{10,1... | collective-permute-start | bytes 196616 | tf_op jit(solution)/shard_map/ppermute | solution.py:28
  277.3 6.5 %collective-permute-start.38 = (f32[128,128]{0,1:T(8,128)S(1)}, f32[128,128]{0,1:T(8,128)S(1)}, u32[]{:S(2)}, u32[]{:S(2)}) collective-permute-start(f32[128,128]{0,1:T(8,128)S(1)} %get-tuple-element.22), channel_id=1, source_target_pairs={{1,0},{2,1},{3,2},{4,3},{5,4},{6,5},{7,6},{8,7},{9,8},{10,9},{11,1... | collective-permute-start | bytes 196616 | tf_op jit(solution)/shard_map/ppermute | solution.py:30
  283.8 6.4 %collective-permute-start.32 = (f32[128,128]{0,1:T(8,128)S(1)}, f32[128,128]{0,1:T(8,128)S(1)}, u32[]{:S(2)}, u32[]{:S(2)}) collective-permute-start(f32[128,128]{0,1:T(8,128)S(1)} %collective-permute-done.31), channel_id=1, source_target_pairs={{0,1},{1,2},{2,3},{3,4},{4,5},{5,6},{6,7},{7,8},{8,9},{9,10},{10,1... | collective-permute-start | bytes 196616 | tf_op jit(solution)/shard_map/ppermute | solution.py:28
  283.8 6.4 %collective-permute-start.39 = (f32[128,128]{0,1:T(8,128)S(1)}, f32[128,128]{0,1:T(8,128)S(1)}, u32[]{:S(2)}, u32[]{:S(2)}) collective-permute-start(f32[128,128]{0,1:T(8,128)S(1)} %collective-permute-done.38), channel_id=1, source_target_pairs={{1,0},{2,1},{3,2},{4,3},{5,4},{6,5},{7,6},{8,7},{9,8},{10,9},{11,1... | collective-permute-start | bytes 196616 | tf_op jit(solution)/shard_map/ppermute | solution.py:30
  290.1 6.4 %collective-permute-start.33 = (f32[128,128]{0,1:T(8,128)S(1)}, f32[128,128]{0,1:T(8,128)S(1)}, u32[]{:S(2)}, u32[]{:S(2)}) collective-permute-start(f32[128,128]{0,1:T(8,128)S(1)} %collective-permute-done.32), channel_id=1, source_target_pairs={{0,1},{1,2},{2,3},{3,4},{4,5},{5,6},{6,7},{7,8},{8,9},{9,10},{10,1... | collective-permute-start | bytes 196616 | tf_op jit(solution)/shard_map/ppermute | solution.py:28
  290.1 6.4 %collective-permute-start.40 = (f32[128,128]{0,1:T(8,128)S(1)}, f32[128,128]{0,1:T(8,128)S(1)}, u32[]{:S(2)}, u32[]{:S(2)}) collective-permute-start(f32[128,128]{0,1:T(8,128)S(1)} %collective-permute-done.39), channel_id=1, source_target_pairs={{1,0},{2,1},{3,2},{4,3},{5,4},{6,5},{7,6},{8,7},{9,8},{10,9},{11,1... | collective-permute-start | bytes 196616 | tf_op jit(solution)/shard_map/ppermute | solution.py:30
  296.5 6.4 %collective-permute-start.34 = (f32[128,128]{0,1:T(8,128)S(1)}, f32[128,128]{0,1:T(8,128)S(1)}, u32[]{:S(2)}, u32[]{:S(2)}) collective-permute-start(f32[128,128]{0,1:T(8,128)S(1)} %collective-permute-done.33), channel_id=1, source_target_pairs={{0,1},{1,2},{2,3},{3,4},{4,5},{5,6},{6,7},{7,8},{8,9},{9,10},{10,1... | collective-permute-start | bytes 196616 | tf_op jit(solution)/shard_map/ppermute | solution.py:28
  296.6 6.4 %collective-permute-start.41 = (f32[128,128]{0,1:T(8,128)S(1)}, f32[128,128]{0,1:T(8,128)S(1)}, u32[]{:S(2)}, u32[]{:S(2)}) collective-permute-start(f32[128,128]{0,1:T(8,128)S(1)} %collective-permute-done.40), channel_id=1, source_target_pairs={{1,0},{2,1},{3,2},{4,3},{5,4},{6,5},{7,6},{8,7},{9,8},{10,9},{11,1... | collective-permute-start | bytes 196616 | tf_op jit(solution)/shard_map/ppermute | solution.py:30
  315.7 15.8 %collective-permute-start.44 = (f32[128,128]{0,1:T(8,128)S(1)}, f32[128,128]{0,1:T(8,128)S(1)}, u32[]{:S(2)}, u32[]{:S(2)}) collective-permute-start(f32[128,128]{0,1:T(8,128)S(1)} %collective-permute-done.43), channel_id=1, source_target_pairs={{1,0},{2,1},{3,2},{4,3},{5,4},{6,5},{7,6},{8,7},{9,8},{10,9},{11,1... | collective-permute-start | bytes 196616 | tf_op jit(solution)/shard_map/ppermute | solution.py:30
  408.7 6.4 %collective-permute-start.45 = (f32[128,128]{0,1:T(8,128)S(1)}, f32[128,128]{0,1:T(8,128)S(1)}, u32[]{:S(2)}, u32[]{:S(2)}) collective-permute-start(f32[128,128]{0,1:T(8,128)S(1)} %get-tuple-element.20), channel_id=1, source_target_pairs={{0,1},{1,2},{2,3},{3,4},{4,5},{5,6},{6,7},{7,8},{8,9},{9,10},{10,1... | collective-permute-start | bytes 196616 | tf_op jit(solution)/shard_map/ppermute | solution.py:28
  415.2 6.5 %collective-permute-start.46 = (f32[128,128]{0,1:T(8,128)S(1)}, f32[128,128]{0,1:T(8,128)S(1)}, u32[]{:S(2)}, u32[]{:S(2)}) collective-permute-start(f32[128,128]{0,1:T(8,128)S(1)} %collective-permute-done.45), channel_id=1, source_target_pairs={{0,1},{1,2},{2,3},{3,4},{4,5},{5,6},{6,7},{7,8},{8,9},{9,10},{10,1... | collective-permute-start | bytes 196616 | tf_op jit(solution)/shard_map/ppermute | solution.py:28
  415.2 6.5 %collective-permute-start.53 = (f32[128,128]{0,1:T(8,128)S(1)}, f32[128,128]{0,1:T(8,128)S(1)}, u32[]{:S(2)}, u32[]{:S(2)}) collective-permute-start(f32[128,128]{0,1:T(8,128)S(1)} %get-tuple-element.20), channel_id=1, source_target_pairs={{1,0},{2,1},{3,2},{4,3},{5,4},{6,5},{7,6},{8,7},{9,8},{10,9},{11,1... | collective-permute-start | bytes 196616 | tf_op jit(solution)/shard_map/ppermute | solution.py:30
  428.1 6.4 %collective-permute-start.55 = (f32[128,128]{0,1:T(8,128)S(1)}, f32[128,128]{0,1:T(8,128)S(1)}, u32[]{:S(2)}, u32[]{:S(2)}) collective-permute-start(f32[128,128]{0,1:T(8,128)S(1)} %collective-permute-done.54), channel_id=1, source_target_pairs={{1,0},{2,1},{3,2},{4,3},{5,4},{6,5},{7,6},{8,7},{9,8},{10,9},{11,1... | collective-permute-start | bytes 196616 | tf_op jit(solution)/shard_map/ppermute | solution.py:30
  434.5 6.5 %collective-permute-start.49 = (f32[128,128]{0,1:T(8,128)S(1)}, f32[128,128]{0,1:T(8,128)S(1)}, u32[]{:S(2)}, u32[]{:S(2)}) collective-permute-start(f32[128,128]{0,1:T(8,128)S(1)} %collective-permute-done.48), channel_id=1, source_target_pairs={{0,1},{1,2},{2,3},{3,4},{4,5},{5,6},{6,7},{7,8},{8,9},{9,10},{10,1... | collective-permute-start | bytes 196616 | tf_op jit(solution)/shard_map/ppermute | solution.py:28
  434.5 7.1 %collective-permute-start.56 = (f32[128,128]{0,1:T(8,128)S(1)}, f32[128,128]{0,1:T(8,128)S(1)}, u32[]{:S(2)}, u32[]{:S(2)}) collective-permute-start(f32[128,128]{0,1:T(8,128)S(1)} %collective-permute-done.55), channel_id=1, source_target_pairs={{1,0},{2,1},{3,2},{4,3},{5,4},{6,5},{7,6},{8,7},{9,8},{10,9},{11,1... | collective-permute-start | bytes 196616 | tf_op jit(solution)/shard_map/ppermute | solution.py:30
  441.6 44.9 %collective-permute-start.57 = (f32[128,128]{0,1:T(8,128)S(1)}, f32[128,128]{0,1:T(8,128)S(1)}, u32[]{:S(2)}, u32[]{:S(2)}) collective-permute-start(f32[128,128]{0,1:T(8,128)S(1)} %collective-permute-done.56), channel_id=1, source_target_pairs={{1,0},{2,1},{3,2},{4,3},{5,4},{6,5},{7,6},{8,7},{9,8},{10,9},{11,1... | collective-permute-start | bytes 196616 | tf_op jit(solution)/shard_map/ppermute | solution.py:30
  447.3 39.1 %collective-permute-start.51 = (f32[128,128]{0,1:T(8,128)S(1)}, f32[128,128]{0,1:T(8,128)S(1)}, u32[]{:S(2)}, u32[]{:S(2)}) collective-permute-start(f32[128,128]{0,1:T(8,128)S(1)} %collective-permute-done.50), channel_id=1, source_target_pairs={{0,1},{1,2},{2,3},{3,4},{4,5},{5,6},{6,7},{7,8},{8,9},{9,10},{10,1... | collective-permute-start | bytes 196616 | tf_op jit(solution)/shard_map/ppermute | solution.py:28
  486.5 6.5 %collective-permute-start.52 = (f32[128,128]{0,1:T(8,128)S(1)}, f32[128,128]{0,1:T(8,128)S(1)}, u32[]{:S(2)}, u32[]{:S(2)}) collective-permute-start(f32[128,128]{0,1:T(8,128)S(1)} %collective-permute-done.51), channel_id=1, source_target_pairs={{0,1},{1,2},{2,3},{3,4},{4,5},{5,6},{6,7},{7,8},{8,9},{9,10},{10,1... | collective-permute-start | bytes 196616 | tf_op jit(solution)/shard_map/ppermute | solution.py:28
  (18 other events, 204.4 us)
Sparse Core Ops, SparseCore 0:
  81.5 59.0 reduce-scatter.3
  211.6 58.3 reduce-scatter.5
  353.2 54.6 reduce-scatter.7
